TPU v7x, 32 devices: a whole 2x2x4 slice. The times are simulated.
32 devices in a mesh: seq: 2 (over y), row: 4 (over x, core), col: 4 (over z).
Axes of the slice: x: 2, y: 2, z: 4, core: 2. Of those that a mesh axis runs over, the one named last changes fastest.
Arguments:
- tokens: bfloat16 [4096, 5376], P(('seq', 'row'), 'col'), may hold values from -6 to 6
- w_query: bfloat16 [5376, 4096], P(('seq', 'row'), 'col'), may hold values from -0.078125 to 0.078125
- key_weight: bfloat16 [5376, 2048], P(('seq', 'row'), 'col'), may hold values from -0.078125 to 0.078125
- value_weight: bfloat16 [5376, 2048], P(('seq', 'row'), 'col'), may hold values from -0.078125 to 0.078125
- w_output: bfloat16 [4096, 5376], P(('seq', 'row'), 'col'), may hold values from -0.09375 to 0.09375
- query_gain: float32 [128], replicated, may hold values from 0.5 to 8
- key_gain: float32 [128], replicated, may hold values from 0.5 to 8
Outputs:
- attended: bfloat16 [4096, 5376], P(('seq', 'row'), 'col')
All inputs are finite; a program needn't handle non-finite values.
Results may differ from a plain program's by a relative error of at most 0.0085.
The roundings to bfloat16 on the way count: a program that leaves them out, or rounds other values in their place, can miss the bound.
Values may be sent and summed in bfloat16 or wider, within the bound.
A program may use at most 128 MiB of HBM per device.

v0:
```python
import jax
import jax.numpy as jnp
from jax import lax
from jax.sharding import PartitionSpec as P

HEAD_SIZE = 128
WINDOW_KEYS = 1024


query_scale = 168.0 ** (-0.5)


def shifted(block, axis, distance):
    devices = range(lax.axis_size(axis))
    route = [(i - distance, i) for i in devices if i - distance in devices]
    return lax.ppermute(block, axis, route)


def head_norm(block, gain):
    mean_square = jnp.mean(block * block, axis=-1, keepdims=True)
    return block * lax.rsqrt(mean_square + 1e-06) * gain


def rotate(block, positions):
    half = block.shape[-1] // 2
    freqs = 10000.0 ** (-(jnp.arange(half, dtype=jnp.float32) * 2.0 / block.shape[-1]))
    angles = positions.astype(jnp.float32)[:, None] * freqs[None, :]
    cosine = jnp.cos(angles)[:, None, :]
    sine = jnp.sin(angles)[:, None, :]
    first = block[..., :half]
    second = block[..., half:]
    return jnp.concatenate(
        [first * cosine - second * sine, second * cosine + first * sine], axis=-1
    )


def attend(queries, key_states, value_states, qpos, kpos):
    rows = queries.shape[0]
    kv_heads = key_states.shape[1]
    grouped = queries.reshape(rows, kv_heads, 2, HEAD_SIZE)
    scores = (
        jnp.einsum("bhgd,khd->hgbk", grouped, key_states, preferred_element_type=jnp.float32)
        * query_scale
    )
    gap = qpos[:, None] - kpos[None, :]
    valid = (kpos[None, :] >= 0) & (gap >= 0) & (gap < WINDOW_KEYS)
    scores = jnp.where(valid[None, None], scores, -1e30)
    top = jnp.max(scores, axis=-1, keepdims=True)
    weights = jnp.exp(scores - top)
    weights = (weights / jnp.sum(weights, axis=-1, keepdims=True)).astype(jnp.bfloat16)
    mixed = jnp.einsum("hgbk,khd->bhgd", weights, value_states, preferred_element_type=jnp.float32)
    return mixed.astype(jnp.bfloat16).reshape(rows, kv_heads * 2 * HEAD_SIZE)


def shards(tokens, w_query, key_weight, value_weight, w_output, query_gain, key_gain):
    rows = tokens.shape[0]
    whole = lax.all_gather(tokens, "col", axis=1, tiled=True)
    columns = whole
    proj_q = jnp.dot(
        columns,
        lax.all_gather(w_query, ("seq", "row"), axis=0, tiled=True),
        preferred_element_type=jnp.float32,
    )
    projected_key = jnp.dot(
        columns,
        lax.all_gather(key_weight, ("seq", "row"), axis=0, tiled=True),
        preferred_element_type=jnp.float32,
    )
    proj_v = jnp.dot(
        columns,
        lax.all_gather(value_weight, ("seq", "row"), axis=0, tiled=True),
        preferred_element_type=jnp.float32,
    )
    base = lax.axis_index(("seq", "row")) * rows
    positions = base + jnp.arange(rows, dtype=jnp.int32)
    q_heads = proj_q.shape[1] // HEAD_SIZE
    kv_heads = projected_key.shape[1] // HEAD_SIZE
    queries = rotate(
        head_norm(proj_q.reshape(rows, q_heads, HEAD_SIZE), query_gain), positions
    ).astype(jnp.bfloat16)
    key_states = rotate(
        head_norm(projected_key.reshape(rows, kv_heads, HEAD_SIZE), key_gain), positions
    ).astype(jnp.bfloat16)
    key_flat = key_states.reshape(rows, kv_heads * HEAD_SIZE)
    value_flat = proj_v.astype(jnp.bfloat16)
    prior_one = shifted((key_flat, value_flat), ("seq", "row"), 1)
    prior_two = shifted((key_flat, value_flat), ("seq", "row"), 2)
    key_rows = jnp.concatenate([prior_two[0], prior_one[0], key_flat], axis=0).reshape(
        3 * rows, kv_heads, HEAD_SIZE
    )
    value_rows = jnp.concatenate([prior_two[1], prior_one[1], value_flat], axis=0).reshape(
        3 * rows, kv_heads, HEAD_SIZE
    )
    kpos = base - 2 * rows + jnp.arange(3 * rows, dtype=jnp.int32)
    mixed = attend(queries, key_rows, value_rows, positions, kpos)
    all_heads = lax.all_gather(mixed, "col", axis=1, tiled=True)
    columns = all_heads
    attended = jnp.dot(
        columns,
        lax.all_gather(w_output, ("seq", "row"), axis=0, tiled=True),
        preferred_element_type=jnp.float32,
    )
    return attended.astype(jnp.bfloat16)


def solution(mesh):
    return jax.shard_map(
        shards,
        mesh=mesh,
        in_specs=(
            P(("seq", "row"), "col"),
            P(("seq", "row"), "col"),
            P(("seq", "row"), "col"),
            P(("seq", "row"), "col"),
            P(("seq", "row"), "col"),
            P(),
            P(),
        ),
        out_specs=P(("seq", "row"), "col"),
        check_vma=False,
    )
```

profile of v0, /device:TPU:17, one launch (start us, length us, event | category | flops | bytes accessed | tf_op | source)
XLA Modules:
  0.0 455.2 jit_solution(17075732382961147357)
XLA Ops:
  6.5 0.0 all-gather.7.cloned.1.call-start
  6.5 0.7 all-gather.7.cloned.1.call-update
  7.3 0.0 all-gather.11.cloned.1.call-start
  7.3 0.7 all-gather.11.cloned.1.call-update
  8.0 0.0 all-gather.9.cloned.1.call-start
  8.1 0.7 all-gather.9.cloned.1.call-update
  8.7 0.0 all-gather.13.cloned.1.call-start
  8.8 0.5 all-gather.13.cloned.1.call-update
  9.3 0.0 all-gather.17.cloned.1.call-start
  9.4 0.5 all-gather.17.cloned.1.call-update
  9.9 0.0 all-gather.15.cloned.1.call-start
  10.0 1.0 multiply_cosine_fusion
  11.0 0.0 copy-start.2
  11.0 99.7 %all-gather.7.cloned.1.call-done = bf16[512,5376]{0,1:T(8,128)(2,1)} async-done(((bf16[512,1344]{0,1:T(8,128)(2,1)}), bf16[512,5376]{0,1:T(8,128)(2,1)}) %all-gather.7.cloned.1.call-update) | async-done | bytes 5505040 | tf_op jit(solution)/shard_map/all_gather | solution.py:57
  110.8 44.5 %all-gather.11.cloned.1.call-done = bf16[5376,512]{1,0:T(8,128)(2,1)} async-done(((bf16[672,512]{1,0:T(8,128)(2,1)}), bf16[5376,512]{1,0:T(8,128)(2,1)}) %all-gather.11.cloned.1.call-update) | async-done | bytes 5505040 | tf_op jit(solution)/shard_map/all_gather | solution.py:66
  155.3 6.7 %multiply_reduce_fusion.1 = (f32[512,4]{0,1:T(4,128)S(1)}, f32[512,512]{0,1:T(8,128)S(1)}) fusion(bf16[512,5376]{0,1:T(8,128)(2,1)} %all-gather.7.cloned.1.call-done, bf16[5376,512]{1,0:T(8,128)(2,1)} %all-gather.11.cloned.1.call-done), kind=kOutput, calls=%fused_computation.29 | convolution fusion | flops 2819094528 | bytes 12066816 | tf_op jit(solution)/shard_map/dot_general | solution.py:64
  162.0 0.3 copy.30
  162.4 0.0 copy-done.2
  162.4 0.3 multiply_multiply_fusion.1
  162.7 0.4 multiply_subtract_fusion
  163.2 0.3 maximum_convert_fusion
  163.5 0.2 copy.31
  163.7 3.1 collective-permute-start.2
  166.8 3.3 collective-permute-start.3
  170.1 37.9 %all-gather.9.cloned.1.call-done = bf16[5376,512]{1,0:T(8,128)(2,1)} async-done(((bf16[672,512]{1,0:T(8,128)(2,1)}), bf16[5376,512]{1,0:T(8,128)(2,1)}) %all-gather.9.cloned.1.call-update) | async-done | bytes 5505040 | tf_op jit(solution)/shard_map/all_gather | solution.py:71
  208.1 7.2 %convolution_convert_fusion.1 = bf16[512,512]{1,0:T(8,128)(2,1)S(1)} fusion(bf16[512,5376]{0,1:T(8,128)(2,1)} %all-gather.7.cloned.1.call-done, bf16[5376,512]{1,0:T(8,128)(2,1)} %all-gather.9.cloned.1.call-done), kind=kOutput, calls=%fused_computation.23 | convolution fusion | flops 2818834432 | bytes 11534336 | tf_op jit(solution)/shard_map/dot_general | solution.py:69
  215.3 3.0 collective-permute-start
  218.3 4.0 collective-permute-start.1
  222.3 2.0 fusion.9
  224.4 0.0 collective-permute-done.2
  224.4 1.0 copy.32
  225.4 0.0 collective-permute-done.3
  225.4 1.0 copy.33
  226.4 11.8 %collective-permute-done = bf16[512,512]{1,0:T(8,128)(2,1)} collective-permute-done((bf16[512,512]{1,0:T(8,128)(2,1)S(1)}, bf16[512,512]{1,0:T(8,128)(2,1)}, u32[]{:S(2)}, u32[]{:S(2)}) %collective-permute-start) | collective-permute-done | bytes 524320 | tf_op jit(solution)/shard_map/ppermute | solution.py:16
  238.2 11.4 %collective-permute-done.1 = bf16[512,512]{1,0:T(8,128)(2,1)} collective-permute-done((bf16[512,512]{1,0:T(8,128)(2,1)S(1)}, bf16[512,512]{1,0:T(8,128)(2,1)}, u32[]{:S(2)}, u32[]{:S(2)}) %collective-permute-start.1) | collective-permute-done | bytes 524320 | tf_op jit(solution)/shard_map/ppermute | solution.py:16
  249.6 1.3 pad_maximum_fusion
  250.9 1.6 copy.43
  252.5 35.4 %all-gather.13.cloned.1.call-done = bf16[5376,1024]{1,0:T(8,128)(2,1)} async-done(((bf16[672,1024]{1,0:T(8,128)(2,1)}), bf16[5376,1024]{1,0:T(8,128)(2,1)}) %all-gather.13.cloned.1.call-update) | async-done | bytes 11010064 | tf_op jit(solution)/shard_map/all_gather | solution.py:61
  287.9 10.3 %convolution_bitcast_fusion = f32[64,8,8,128]{3,1,2,0:T(8,128)S(1)} fusion(bf16[512,5376]{0,1:T(8,128)(2,1)} %all-gather.7.cloned.1.call-done, bf16[5376,1024]{1,0:T(8,128)(2,1)} %all-gather.13.cloned.1.call-done), kind=kOutput, calls=%fused_computation.19 | convolution fusion | flops 5637144576 | bytes 18612224 | tf_op jit(solution)/shard_map/dot_general | solution.py:59
  298.2 0.0 copy-start.3
  298.2 0.5 copy.44
  298.7 0.6 multiply_reduce_fusion
  299.3 0.1 copy.34
  299.4 0.1 copy.35
  299.5 0.0 copy-done.3
  299.6 0.9 multiply_multiply_fusion
  300.4 0.9 subtract_convert_fusion
  301.3 0.0 copy-start
  301.3 0.0 copy-start.1
  301.3 0.1 copy.37
  301.5 0.1 copy.36
  301.6 0.8 copy-done
  302.4 0.2 copy-done.1
  302.5 11.8 %fusion.11 = f32[4,1536,512,2]{2,1,3,0:T(8,128)} fusion(bf16[512,4,128]{2,0,1:T(8,128)(2,1)S(1)} %maximum_convert_fusion, bf16[512,4,128]{2,0,1:T(8,128)(2,1)S(1)} %copy-done.1, bf16[512,4,128]{2,0,1:T(8,128)(2,1)S(1)} %copy-done, bf16[512,4,2,64]{3,0,2,1:T(8,128)(2,1)S(1)} %bitcast.51, bf16[512,4,2,64]{3,0,2,1:T(8,128)(2,1)S(1)} %bitcast.53), kind=kOutput, calls=%fused_computation.30 | convolution fusion | flops 1617428480 | bytes 27787264 | tf_op jit(solution)/shard_map/bhgd,khd->hgbk/dot_general | solution.py:42
  314.4 10.5 %fusion.23 = f32[4,2,512]{2,1,0:T(2,128)S(1)} fusion(pred[512,1536]{0,1:T(8,128)(4,1)} %fusion.9, bf16[512,4,128]{2,0,1:T(8,128)(2,1)S(1)} %maximum_convert_fusion, bf16[512,4,128]{2,0,1:T(8,128)(2,1)} %copy.33, bf16[512,4,128]{2,0,1:T(8,128)(2,1)S(1)} %copy-done, bf16[512,4,2,64]{3,0,2,1:T(8,128)(2,1)S(1)} %bitcast.52, bf16[512,4,2,64]{3,0,2,1:T(8,128)(2,1)S(1)} %bitcast.54), kind=kOutput, calls=%fused_computation.47 | convolution fusion | flops 1642595840 | bytes 3424256 | tf_op jit(solution)/shard_map/sub | solution.py:49
  324.9 15.4 %fusion.10 = bf16[4,128,2,512]{3,1,2,0:T(8,128)(2,1)} fusion(bf16[1536,4,128,1]{0,2,3,1:T(8,128)(2,1)} %bitcast.55, f32[4,2,512]{2,1,0:T(2,128)S(1)} %fusion.23, f32[4,1536,512,2]{2,1,3,0:T(8,128)} %fusion.11, pred[512,1536]{0,1:T(8,128)(4,1)} %fusion.9), kind=kOutput, calls=%fused_computation.22 | convolution fusion | flops 1642599936 | bytes 28590080 | tf_op jit(solution)/shard_map/hgbk,khd->bhgd/dot_general | solution.py:51
  340.3 0.0 all-gather.15.cloned.1.call-update
  340.3 17.0 %all-gather.17.cloned.1.call-done = bf16[4096,1344]{0,1:T(8,128)(2,1)} async-done(((bf16[512,1344]{0,1:T(8,128)(2,1)}), bf16[4096,1344]{0,1:T(8,128)(2,1)}) %all-gather.17.cloned.1.call-update) | async-done | bytes 11010064 | tf_op jit(solution)/shard_map/all_gather | solution.py:100
  357.3 80.3 %all-gather.15.cloned.1.call-done = bf16[512,4096]{0,1:T(8,128)(2,1)} async-done(((bf16[512,1024]{0,1:T(8,128)(2,1)}), bf16[512,4096]{0,1:T(8,128)(2,1)}) %all-gather.15.cloned.1.call-update) | async-done | bytes 4194320 | tf_op jit(solution)/shard_map/all_gather | solution.py:96
  437.6 10.7 %convolution_convert_fusion = bf16[512,1344]{0,1:T(8,128)(2,1)} fusion(bf16[4096,1344]{0,1:T(8,128)(2,1)} %all-gather.17.cloned.1.call-done, bf16[512,4096]{0,1:T(8,128)(2,1)} %all-gather.15.cloned.1.call-done), kind=kOutput, calls=%fused_computation.14 | convolution fusion | flops 5637832704 | bytes 16580608 | tf_op jit(solution)/shard_map/dot_general | solution.py:98
  (7 shorter events, 0.1 us)
Async XLA Ops:
  6.5 104.2 %all-gather.7.cloned.1.call-start = ((), (), s32[]{:S(2)}) async-start(), calls=%async_computation | async-start | bytes 6881280 | tf_op jit(solution)/shard_map/all_gather | solution.py:57
  7.3 148.1 %all-gather.11.cloned.1.call-start = ((), (), s32[]{:S(2)}) async-start(), calls=%async_computation.2 | async-start | bytes 6193152 | tf_op jit(solution)/shard_map/all_gather | solution.py:66
  8.0 200.0 %all-gather.9.cloned.1.call-start = ((), (), s32[]{:S(2)}) async-start(), calls=%async_computation.1 | async-start | bytes 6193152 | tf_op jit(solution)/shard_map/all_gather | solution.py:71
  8.7 279.2 %all-gather.13.cloned.1.call-start = ((), (), s32[]{:S(2)}) async-start(), calls=%async_computation.3 | async-start | bytes 12386304 | tf_op jit(solution)/shard_map/all_gather | solution.py:61
  9.3 348.0 %all-gather.17.cloned.1.call-start = ((), (), s32[]{:S(2)}) async-start(), calls=%async_computation.5 | async-start | bytes 12386304 | tf_op jit(solution)/shard_map/all_gather | solution.py:100
  9.9 427.7 %all-gather.15.cloned.1.call-start = ((), (), s32[]{:S(2)}) async-start(), calls=%async_computation.4 | async-start | bytes 5242880 | tf_op jit(solution)/shard_map/all_gather | solution.py:96
  11.0 151.4 %copy-start.2 = (f32[128]{0:T(128)S(1)}, f32[128]{0:T(128)}, u32[]{:S(2)}) copy-start(f32[128]{0:T(128)} %param.13) | copy-start | bytes 1540
  163.7 60.6 %collective-permute-start.2 = (bf16[512,512]{0,1:T(8,128)(2,1)S(1)}, bf16[512,512]{0,1:T(8,128)(2,1)S(1)}, u32[]{:S(2)}, u32[]{:S(2)}) collective-permute-start(bf16[512,512]{0,1:T(8,128)(2,1)S(1)} %bitcast.58), channel_id=1, source_target_pairs={{0,8},{4,12},{8,16},{12,20},{16,24},{20,28},{1,9},{5,13},{9,17},{1... | collective-permute-start | bytes 1572872 | tf_op jit(solution)/shard_map/ppermute | solution.py:16
  166.8 58.5 %collective-permute-start.3 = (bf16[512,512]{0,1:T(8,128)(2,1)S(1)}, bf16[512,512]{0,1:T(8,128)(2,1)S(1)}, u32[]{:S(2)}, u32[]{:S(2)}) collective-permute-start(bf16[512,512]{0,1:T(8,128)(2,1)S(1)} %bitcast.59), channel_id=1, source_target_pairs={{0,4},{4,8},{8,12},{12,16},{16,20},{20,24},{24,28},{1,5},{5,9},{9,... | collective-permute-start | bytes 1572872 | tf_op jit(solution)/shard_map/ppermute | solution.py:16
  215.3 22.9 %collective-permute-start = (bf16[512,512]{1,0:T(8,128)(2,1)S(1)}, bf16[512,512]{1,0:T(8,128)(2,1)}, u32[]{:S(2)}, u32[]{:S(2)}) collective-permute-start(bf16[512,512]{1,0:T(8,128)(2,1)S(1)} %convolution_convert_fusion.1), channel_id=1, source_target_pairs={{0,8},{4,12},{8,16},{12,20},{16,24},{20,28},{1,9},{5,13},{9,17},{1... | collective-permute-start | bytes 1572872 | tf_op jit(solution)/shard_map/ppermute | solution.py:16
  218.3 31.3 %collective-permute-start.1 = (bf16[512,512]{1,0:T(8,128)(2,1)S(1)}, bf16[512,512]{1,0:T(8,128)(2,1)}, u32[]{:S(2)}, u32[]{:S(2)}) collective-permute-start(bf16[512,512]{1,0:T(8,128)(2,1)S(1)} %convolution_convert_fusion.1), channel_id=1, source_target_pairs={{0,4},{4,8},{8,12},{12,16},{16,20},{20,24},{24,28},{1,5},{5,9},{9,... | collective-permute-start | bytes 1572872 | tf_op jit(solution)/shard_map/ppermute | solution.py:16
  298.2 1.4 copy-start.3
  301.3 1.1 copy-start
  301.3 1.2 copy-start.1
Sparse Core Ops, SparseCore 0:
  8.9 101.7 all-gather.6
  112.6 42.6 all-gather.10
  157.2 50.8 all-gather.8
  209.8 78.0 all-gather.12
  289.6 67.6 all-gather.16
  358.7 78.8 all-gather.14
where the time goes:
time: 458 us; the launch traced here: 455 us
  waiting for transfers between devices  341 us (74%)
  matrix products  72.6 us (16%)
  between operations  13.7 us (3%)
  starting transfers between devices  13.6 us (3%)
  other arithmetic  7.77 us (2%)
  local copies, waits for them, and re-layouts  6.04 us (1%)
    all_gather x1, waiting for transfers between devices, shards(): whole = lax.all_gather(tokens, 'col', axis=1, tiled=True)  99.7 us
    all_gather x1, waiting for transfers between devices, shards(): all_heads = lax.all_gather(mixed, 'col', axis=1, tiled=True)  80.3 us
    all_gather x1, waiting for transfers between devices, shards(): lax.all_gather(key_weight, ('seq', 'row'), axis=0, tiled=True)  44.5 us
    all_gather x1, waiting for transfers between devices, shards(): lax.all_gather(value_weight, ('seq', 'row'), axis=0, tiled=True)  37.9 us
    all_gather x1, waiting for transfers between devices, shards(): lax.all_gather(w_query, ('seq', 'row'), axis=0, tiled=True)  35.4 us
    ppermute x4, waiting for transfers between devices, shifted(): return lax.ppermute(block, axis, route)  23.2 us
    all_gather x1, waiting for transfers between devices, shards(): lax.all_gather(w_output, ('seq', 'row'), axis=0, tiled=True)  17 us
    dot_general x1, matrix products, attend(): jnp.einsum('hgbk,khd->bhgd', weights, value_states, preferred_element_typ...  15.4 us
  transfers between devices with their start and end apart: 10, of which 8 were waited for; matrix products, arithmetic and copies ran while one was open for 16% of the time, Pallas kernels for 0%

commit v1 on v0

--- a/solution.py
+++ b/solution.py
@@ -1,6 +1,8 @@
 import jax
 import jax.numpy as jnp
 from jax import lax
+from jax.experimental import pallas as pl
+from jax.experimental.pallas import tpu as pltpu
 from jax.sharding import PartitionSpec as P
 
 HEAD_SIZE = 128
@@ -103,19 +105,347 @@
     return attended.astype(jnp.bfloat16)
 
 
+MESH = pl.DeviceIdType.MESH
+MIB = 1 << 20
+
+
+class Place:
+    def __init__(self):
+        self.y = lax.axis_index("seq")
+        row = lax.axis_index("row")
+        self.x, self.c = row // 2, row % 2
+        self.z = lax.axis_index("col")
+        self.to_x = {"seq": self.y, "row": (1 - self.x) * 2 + self.c, "col": self.z}
+        self.to_y = {"seq": 1 - self.y, "row": row, "col": self.z}
+        self.to_c = {"seq": self.y, "row": self.x * 2 + 1 - self.c, "col": self.z}
+        self.up = {"seq": self.y, "row": row, "col": self.z + 1}
+        self.down = {"seq": self.y, "row": row, "col": self.z - 1}
+        self.chip = self.y * 2 + self.x
+        self.chip_x = self.y * 2 + 1 - self.x
+        self.chip_y = (1 - self.y) * 2 + self.x
+        self.chip_d = (1 - self.y) * 2 + 1 - self.x
+
+
+def barrier(at):
+    sem = pltpu.get_barrier_semaphore()
+    for device in (at.to_x, at.to_y, at.to_c):
+        pl.semaphore_signal(sem, inc=1, device_id=device, device_id_type=MESH)
+
+    @pl.when(at.z < 3)
+    def _():
+        pl.semaphore_signal(sem, inc=1, device_id=at.up, device_id_type=MESH)
+
+    @pl.when(at.z > 0)
+    def _():
+        pl.semaphore_signal(sem, inc=1, device_id=at.down, device_id_type=MESH)
+
+    peers = 3 + (at.z < 3).astype(jnp.int32) + (at.z > 0).astype(jnp.int32)
+    pl.semaphore_wait(sem, peers)
+
+
+class Line:
+    def __init__(self, at, buf, send, recv):
+        self.at, self.buf, self.send, self.recv = at, buf, send, recv
+        self.half = buf.shape[1] // 2
+
+    def copy(self, block, half, way):
+        part = self.buf.at[block, pl.ds(half * self.half, self.half)]
+        return pltpu.make_async_remote_copy(
+            src_ref=part, dst_ref=part,
+            send_sem=self.send.at[way, block, half], recv_sem=self.recv.at[block, half],
+            device_id=self.at.up if way == 0 else self.at.down, device_id_type=MESH)
+
+    def start(self, half):
+        at = self.at
+
+        @pl.when(at.z < 3)
+        def _():
+            self.copy(at.z, half, 0).start()
+
+        @pl.when(at.z > 0)
+        def _():
+            self.copy(at.z, half, 1).start()
+
+    def step(self, s, half):
+        at = self.at
+
+        @pl.when(at.z - s >= 0)
+        def _():
+            self.copy(at.z - s, half, 0).wait_recv()
+
+            @pl.when(at.z < 3)
+            def _():
+                self.copy(at.z - s, half, 0).start()
+
+        @pl.when(at.z + s <= 3)
+        def _():
+            self.copy(at.z + s, half, 1).wait_recv()
+
+            @pl.when(at.z > 0)
+            def _():
+                self.copy(at.z + s, half, 1).start()
+
+    def finish(self, half):
+        at = self.at
+        for s in range(4):
+            @pl.when((at.z - s >= 0) & (at.z < 3))
+            def _():
+                self.copy(at.z - s, half, 0).wait_send()
+
+            @pl.when((at.z + s <= 3) & (at.z > 0))
+            def _():
+                self.copy(at.z + s, half, 1).wait_send()
+
+
+class Plane:
+    def __init__(self, at, buf, send, recv):
+        self.at, self.buf, self.send, self.recv = at, buf, send, recv
+        self.rows = buf.shape[0] // 8
+        self.half = self.rows // 2
+        self.sent = []
+
+    def copy(self, chip, core, half, device, slot):
+        start = pl.multiple_of((chip * 2 + core) * self.rows + half * self.half, 16)
+        part = self.buf.at[pl.ds(start, self.half)]
+        return pltpu.make_async_remote_copy(
+            src_ref=part, dst_ref=part,
+            send_sem=self.send.at[slot], recv_sem=self.recv.at[chip * 2 + core, half],
+            device_id=device, device_id_type=MESH)
+
+    def push(self, chip, half, device):
+        one = self.copy(chip, self.at.c, half, device, len(self.sent))
+        one.start()
+        self.sent.append(one)
+
+    def need(self, chip, core, half):
+        self.copy(chip, core, half, self.at.to_c, 0).wait_recv()
+
+    def start(self):
+        at = self.at
+        self.push(at.chip, 0, at.to_x)
+        self.push(at.chip, 1, at.to_y)
+        self.push(at.chip, 1, at.to_x)
+        self.push(at.chip, 0, at.to_y)
+        self.push(at.chip, 0, at.to_c)
+        self.push(at.chip, 1, at.to_c)
+
+    def first(self):
+        at = self.at
+        self.need(at.chip_x, at.c, 0)
+        self.push(at.chip_x, 0, at.to_y)
+        self.push(at.chip_x, 0, at.to_c)
+        self.need(at.chip_y, at.c, 1)
+        self.push(at.chip_y, 1, at.to_x)
+        self.push(at.chip_y, 1, at.to_c)
+
+    def second(self):
+        at = self.at
+        self.need(at.chip_x, at.c, 1)
+        self.push(at.chip_x, 1, at.to_c)
+        self.need(at.chip_y, at.c, 0)
+        self.push(at.chip_y, 0, at.to_c)
+        for half in range(2):
+            self.need(at.chip, 1 - at.c, half)
+            self.need(at.chip_x, 1 - at.c, half)
+            self.need(at.chip_y, 1 - at.c, half)
+
+    def third(self):
+        at = self.at
+        for half in range(2):
+            self.need(at.chip_d, at.c, half)
+            self.push(at.chip_d, half, at.to_c)
+        for half in range(2):
+            self.need(at.chip_d, 1 - at.c, half)
+
+    def finish(self):
+        for one in self.sent:
+            one.wait_send()
+
+
+SENDS = 14
+
+
+def multiply(chunk, x_all, w_all, total):
+    depth = x_all.shape[2]
+    width = total.shape[1]
+    rows = pl.ds(pl.multiple_of(chunk * depth, 32), depth)
+    tiles = width // 256
+
+    @pl.loop(0, tiles)
+    def _(tile):
+        cols = pl.ds(pl.multiple_of(tile * 256, 256), 256)
+        total[:, cols] += jnp.dot(
+            x_all[chunk], w_all[rows, cols], preferred_element_type=jnp.float32)
+
+    if width % 256:
+        rest = pl.ds(tiles * 256, width % 256)
+        total[:, rest] += jnp.dot(
+            x_all[chunk], w_all[rows, rest], preferred_element_type=jnp.float32)
+
+
+def gather_multiply(at, line, plane, total):
+    late = lambda j: (j == at.chip_d) | (j - at.z == 3) | (at.z - j == 3)
+    line.start(0)
+    plane.start()
+    line.start(1)
+    total[...] = jnp.zeros_like(total)
+    line.step(1, 0)
+    plane.first()
+    line.step(1, 1)
+    line.step(2, 0)
+    line.step(2, 1)
+    plane.second()
+
+    @pl.loop(0, 4)
+    def _(j):
+        @pl.when(jnp.logical_not(late(j)))
+        def _():
+            multiply(j, line.buf, plane.buf, total)
+
+    line.step(3, 0)
+    line.step(3, 1)
+    plane.third()
+
+    @pl.loop(0, 4)
+    def _(j):
+        @pl.when(late(j))
+        def _():
+            multiply(j, line.buf, plane.buf, total)
+
+
+def finish(line, plane):
+    line.finish(0)
+    line.finish(1)
+    plane.finish()
+
+
+def project_kernel(x, wq, wk, wv, gains, cosine, sine, q, k, v,
+                   x_all, w_all, total, zs, zr, ps, pr, local):
+    at = Place()
+    shard = w_all.shape[0] // 8
+    nq, nk = wq.shape[1], wk.shape[1]
+    mine = pl.ds(pl.multiple_of((at.chip * 2 + at.c) * shard, 16), shard)
+    loads = [
+        pltpu.make_async_copy(x, x_all.at[at.z], local.at[0]),
+        pltpu.make_async_copy(wq, w_all.at[mine, pl.ds(0, nq)], local.at[1]),
+        pltpu.make_async_copy(wk, w_all.at[mine, pl.ds(nq, nk)], local.at[2]),
+        pltpu.make_async_copy(wv, w_all.at[mine, pl.ds(nq + nk, nk)], local.at[3]),
+    ]
+    for load in loads:
+        load.start()
+    barrier(at)
+    for load in loads:
+        load.wait()
+    line, plane = Line(at, x_all, zs, zr), Plane(at, w_all, ps, pr)
+    gather_multiply(at, line, plane, total)
+
+    def head(col, gain):
+        block = total[:, pl.ds(pl.multiple_of(col, 128), 128)]
+        mean_square = jnp.mean(block * block, axis=-1, keepdims=True)
+        normed = block * lax.rsqrt(mean_square + 1e-06) * gain
+        turned = normed * cosine[...] + pltpu.roll(normed, 64, 1) * sine[...]
+        return turned.astype(jnp.bfloat16)
+
+    @pl.loop(0, nq // 128)
+    def _(h):
+        q[:, pl.ds(pl.multiple_of(h * 128, 128), 128)] = head(h * 128, gains[0:1, :])
+
+    @pl.loop(0, nk // 128)
+    def _(h):
+        k[:, pl.ds(pl.multiple_of(h * 128, 128), 128)] = head(nq + h * 128, gains[1:2, :])
+
+    v[...] = total[:, nq + nk:].astype(jnp.bfloat16)
+    finish(line, plane)
+
+
+def output_kernel(x, w, out, x_all, w_all, total, zs, zr, ps, pr, local):
+    at = Place()
+    shard = w_all.shape[0] // 8
+    mine = pl.ds(pl.multiple_of((at.chip * 2 + at.c) * shard, 16), shard)
+    loads = [
+        pltpu.make_async_copy(x, x_all.at[at.z], local.at[0]),
+        pltpu.make_async_copy(w, w_all.at[mine], local.at[1]),
+    ]
+    for load in loads:
+        load.start()
+    barrier(at)
+    for load in loads:
+        load.wait()
+    line, plane = Line(at, x_all, zs, zr), Plane(at, w_all, ps, pr)
+    gather_multiply(at, line, plane, total)
+    out[...] = total[...].astype(jnp.bfloat16)
+    finish(line, plane)
+
+
+def gather_scratch(rows, depth, width):
+    return [
+        pltpu.VMEM((4, rows, depth), jnp.bfloat16),
+        pltpu.VMEM((4 * depth, width), jnp.bfloat16),
+        pltpu.VMEM((rows, width), jnp.float32),
+        pltpu.SemaphoreType.DMA((2, 4, 2)),
+        pltpu.SemaphoreType.DMA((4, 2)),
+        pltpu.SemaphoreType.DMA((SENDS,)),
+        pltpu.SemaphoreType.DMA((8, 2)),
+        pltpu.SemaphoreType.DMA((4,)),
+    ]
+
+
+HBM = pl.BlockSpec(memory_space=pl.ANY)
+LOCAL = pl.BlockSpec(memory_space=pltpu.VMEM)
+
+
+def angles_of(positions):
+    freqs = 10000.0 ** (-(jnp.arange(64, dtype=jnp.float32) * 2.0 / HEAD_SIZE))
+    angles = positions.astype(jnp.float32)[:, None] * freqs[None, :]
+    cosine, sine = jnp.cos(angles), jnp.sin(angles)
+    return jnp.concatenate([cosine, cosine], 1), jnp.concatenate([-sine, sine], 1)
+
+
+def fused(tokens, w_query, key_weight, value_weight, w_output, query_gain, key_gain):
+    rows, depth = tokens.shape
+    nq, nk = w_query.shape[1], key_weight.shape[1]
+    base = lax.axis_index(("seq", "row")) * rows
+    positions = base + jnp.arange(rows, dtype=jnp.int32)
+    cosine, sine = angles_of(positions)
+    gains = jnp.stack([query_gain, key_gain])
+    bf16 = jnp.bfloat16
+    queries, key_flat, value_flat = pl.pallas_call(
+        project_kernel,
+        out_shape=[jax.ShapeDtypeStruct((rows, n), bf16) for n in (nq, nk, nk)],
+        in_specs=[HBM] * 4 + [LOCAL] * 3,
+        out_specs=[LOCAL] * 3,
+        scratch_shapes=gather_scratch(rows, depth, nq + 2 * nk),
+        compiler_params=pltpu.CompilerParams(
+            collective_id=0, has_side_effects=True, vmem_limit_bytes=56 * MIB),
+    )(tokens, w_query, key_weight, value_weight, gains, cosine, sine)
+    kv_heads = nk // HEAD_SIZE
+    one = shifted((key_flat, value_flat), ("seq", "row"), 1)
+    two = shifted((key_flat, value_flat), ("seq", "row"), 2)
+    key_rows = jnp.concatenate([two[0], one[0], key_flat], 0)
+    value_rows = jnp.concatenate([two[1], one[1], value_flat], 0)
+    kpos = base - 2 * rows + jnp.arange(3 * rows, dtype=jnp.int32)
+    mixed = attend(
+        queries.reshape(rows, nq // HEAD_SIZE, HEAD_SIZE),
+        key_rows.reshape(3 * rows, kv_heads, HEAD_SIZE),
+        value_rows.reshape(3 * rows, kv_heads, HEAD_SIZE), positions, kpos)
+    return pl.pallas_call(
+        output_kernel,
+        out_shape=jax.ShapeDtypeStruct((rows, w_output.shape[1]), bf16),
+        in_specs=[HBM] * 2,
+        out_specs=LOCAL,
+        scratch_shapes=gather_scratch(rows, nq, w_output.shape[1]),
+        compiler_params=pltpu.CompilerParams(
+            collective_id=1, has_side_effects=True, vmem_limit_bytes=48 * MIB),
+    )(mixed, w_output)
+
+
 def solution(mesh):
+    small = dict(mesh.shape) == {"seq": 2, "row": 4, "col": 4}
+    split = P(("seq", "row"), "col")
     return jax.shard_map(
-        shards,
+        fused if small else shards,
         mesh=mesh,
-        in_specs=(
-            P(("seq", "row"), "col"),
-            P(("seq", "row"), "col"),
-            P(("seq", "row"), "col"),
-            P(("seq", "row"), "col"),
-            P(("seq", "row"), "col"),
-            P(),
-            P(),
-        ),
-        out_specs=P(("seq", "row"), "col"),
+        in_specs=(split, split, split, split, split, P(), P()),
+        out_specs=split,
         check_vma=False,
     )

time: 458 us -> 277 us (0.60)
  the two profiles are of different devices: /device:TPU:17 before, /device:TPU:5 now
where the time goes in v1:
time: 277 us
  Pallas kernels  197 us (71%)
  matrix products  37.9 us (14%)
  local copies, waits for them, and re-layouts  13.5 us (5%)
  waiting for transfers between devices  11.6 us (4%)
  starting transfers between devices  9.2 us (3%)
  other arithmetic  7.2 us (3%)
    pallas_call x1, Pallas kernels, fused(): pl.pallas_call(project_kernel, out_shape=[jax.ShapeDtypeStruct((rows, n),...  118 us
    pallas_call x1, Pallas kernels, fused(): pl.pallas_call(output_kernel, out_shape=jax.ShapeDtypeStruct((rows, w_out...  79.6 us
    dot_general x1, matrix products, attend(): jnp.einsum('hgbk,khd->bhgd', weights, value_states, preferred_element_typ...  14.2 us
    dot_general x1, matrix products, attend(): jnp.einsum('bhgd,khd->hgbk', grouped, key_states, preferred_element_type=...  13 us
    ppermute x4, waiting for transfers between devices, shifted(): return lax.ppermute(block, axis, route)  11.6 us
    sub x1, matrix products, attend(): weights = jnp.exp(scores - top)  10.6 us
    ppermute x4, starting transfers between devices, shifted(): return lax.ppermute(block, axis, route)  9.2 us
  transfers between devices with their start and end apart: 4, of which 2 were waited for; matrix products, arithmetic and copies ran while one was open for 12% of the time, Pallas kernels for 0%

profile of v1, /device:TPU:5, one launch (start us, length us, event | category | flops | bytes accessed | tf_op | source)
XLA Modules:
  0.0 276.9 jit_solution(5960586721558524504)
XLA Ops:
  0.0 0.0 copy-start.6
  0.0 0.0 copy-start.5
  0.0 2.5 copy.8.x
  2.6 1.0 fusion.18
  3.6 0.0 copy-done.6
  3.6 0.0 copy-done.5
  3.6 0.5 pad_maximum_fusion.4.gains
  4.1 1.0 pad_maximum_fusion.2
  5.1 0.0 copy-start.2
  5.1 117.8 %shard_map.73 = (bf16[512,1024]{1,0:T(8,128)(2,1)}, bf16[512,512]{1,0:T(8,128)(2,1)}, bf16[512,512]{1,0:T(8,128)(2,1)}) custom-call(bf16[512,1344]{1,0:T(8,128)(2,1)} %copy.8.x, bf16[672,1024]{1,0:T(8,128)(2,1)} %wq.1, bf16[672,512]{1,0:T(8,128)(2,1)} %wk.1, bf16[672,512]{1,0:T(8,128)(2,1)} %wv.1, f32[2,128]{1,0:T(2,128)} %pad_maximum_fusion.4.gains, ...), custom_call_target="tpu_custom_call" | custom-call | tf_op jit(solution)/shard_map/pallas_call | solution.py:412
  122.9 0.0 copy-start.4
  122.9 3.2 %collective-permute-start.2 = (bf16[512,512]{1,0:T(8,128)(2,1)}, bf16[512,512]{1,0:T(8,128)(2,1)}, u32[]{:S(2)}, u32[]{:S(2)}) collective-permute-start(bf16[512,512]{1,0:T(8,128)(2,1)} %get-tuple-element.9), channel_id=1, source_target_pairs={{0,8},{4,12},{8,16},{12,20},{16,24},{20,28},{1,9},{5,13},{9,17},{1... | collective-permute-start | bytes 1572872 | tf_op jit(solution)/shard_map/ppermute | solution.py:18
  126.2 1.9 collective-permute-start.3
  128.1 1.9 collective-permute-start
  130.0 2.1 collective-permute-start.1
  132.2 2.6 reshape_reshape.3
  134.7 0.0 copy-done.2
  134.7 0.8 copy.14.w
  135.6 2.0 fusion.9
  137.6 2.5 collective-permute-done.2
  140.1 9.1 %collective-permute-done.3 = bf16[512,512]{1,0:T(8,128)(2,1)} collective-permute-done((bf16[512,512]{1,0:T(8,128)(2,1)}, bf16[512,512]{1,0:T(8,128)(2,1)}, u32[]{:S(2)}, u32[]{:S(2)}) %collective-permute-start.3) | collective-permute-done | bytes 524320 | tf_op jit(solution)/shard_map/ppermute | solution.py:18
  149.2 0.0 copy-done.4
  149.2 1.3 pad_maximum_fusion.1
  150.5 1.9 reshape.78
  152.4 0.0 copy-start.1
  152.4 10.6 %fusion.27 = f32[4,2,512]{2,1,0:T(2,128)S(1)} fusion(pred[512,1536]{0,1:T(8,128)(4,1)} %fusion.9, bf16[1536,4,128,1]{2,1,0,3:T(4,128)(2,1)} %bitcast.25, bf16[512,4,2,128]{3,2,1,0:T(2,128)(2,1)} %reshape_reshape.3), kind=kOutput, calls=%fused_computation.38 | convolution fusion | flops 1635780096 | bytes 3424256 | tf_op jit(solution)/shard_map/sub | solution.py:51
  163.0 0.0 copy-done.1
  163.0 0.0 copy-start.3
  163.0 13.0 %fusion.13 = f32[4,1536,512,2]{2,1,3,0:T(8,128)} fusion(bf16[1536,4,128,1]{2,1,0,3:T(4,128)(2,1)S(1)} %bitcast.26, bf16[512,4,2,128]{3,2,1,0:T(2,128)(2,1)} %reshape_reshape.3), kind=kOutput, calls=%fused_computation.18 | convolution fusion | flops 1610612736 | bytes 27787264 | tf_op jit(solution)/shard_map/bhgd,khd->hgbk/dot_general | solution.py:44
  176.0 0.0 collective-permute-done
  176.0 0.0 collective-permute-done.1
  176.0 0.0 copy-done.3
  176.0 1.3 pad_maximum_fusion
  177.4 1.6 copy.19
  179.0 14.2 %fusion.10 = bf16[4,128,2,512]{3,1,2,0:T(8,128)(2,1)S(1)} fusion(bf16[1536,4,128,1]{0,2,3,1:T(8,128)(2,1)} %bitcast.27, f32[4,2,512]{2,1,0:T(2,128)S(1)} %fusion.27, f32[4,1536,512,2]{2,1,3,0:T(8,128)} %fusion.13, pred[512,1536]{0,1:T(8,128)(4,1)} %fusion.9), kind=kOutput, calls=%fused_computation.16 | convolution fusion | flops 1642599936 | bytes 28590080 | tf_op jit(solution)/shard_map/hgbk,khd->bhgd/dot_general | solution.py:53
  193.2 1.3 copy.22.x
  194.5 0.0 copy-start
  194.5 1.2 copy-done
  195.7 79.6 %shard_map.74 = bf16[512,1344]{1,0:T(8,128)(2,1)S(1)} custom-call(bf16[512,1024]{1,0:T(8,128)(2,1)S(1)} %copy-done, bf16[512,1344]{1,0:T(8,128)(2,1)S(1)} %copy.14.w), custom_call_target="tpu_custom_call" | custom-call | tf_op jit(solution)/shard_map/pallas_call | solution.py:431
  275.4 1.5 copy.15
  (5 shorter events, 0.0 us)
Async XLA Ops:
  0.0 3.6 %copy-start.6 = (f32[128]{0:T(128)S(1)}, f32[128]{0:T(128)}, u32[]{:S(2)}) copy-start(f32[128]{0:T(128)} %param.12) | copy-start | bytes 1540
  0.0 3.6 %copy-start.5 = (f32[128]{0:T(128)S(1)}, f32[128]{0:T(128)}, u32[]{:S(2)}) copy-start(f32[128]{0:T(128)} %param.13) | copy-start | bytes 1540
  5.1 129.6 %copy-start.2 = (bf16[512,1344]{0,1:T(8,128)(2,1)S(1)}, bf16[512,1344]{0,1:T(8,128)(2,1)}, u32[]{:S(2)}) copy-start(bf16[512,1344]{0,1:T(8,128)(2,1)} %param.11) | copy-start | bytes 4128772
  122.9 26.3 %copy-start.4 = (bf16[512,512]{1,0:T(8,128)(2,1)S(1)}, bf16[512,512]{1,0:T(8,128)(2,1)}, u32[]{:S(2)}) copy-start(bf16[512,512]{1,0:T(8,128)(2,1)} %get-tuple-element.9) | copy-start | bytes 1572868
  122.9 17.2 %collective-permute-start.2 = (bf16[512,512]{1,0:T(8,128)(2,1)}, bf16[512,512]{1,0:T(8,128)(2,1)}, u32[]{:S(2)}, u32[]{:S(2)}) collective-permute-start(bf16[512,512]{1,0:T(8,128)(2,1)} %get-tuple-element.9), channel_id=1, source_target_pairs={{0,8},{4,12},{8,16},{12,20},{16,24},{20,28},{1,9},{5,13},{9,17},{1... | collective-permute-start | bytes 1572872 | tf_op jit(solution)/shard_map/ppermute | solution.py:18
  126.2 23.0 %collective-permute-start.3 = (bf16[512,512]{1,0:T(8,128)(2,1)}, bf16[512,512]{1,0:T(8,128)(2,1)}, u32[]{:S(2)}, u32[]{:S(2)}) collective-permute-start(bf16[512,512]{1,0:T(8,128)(2,1)} %get-tuple-element.9), channel_id=1, source_target_pairs={{0,4},{4,8},{8,12},{12,16},{16,20},{20,24},{24,28},{1,5},{5,9},{9,... | collective-permute-start | bytes 1572872 | tf_op jit(solution)/shard_map/ppermute | solution.py:18
  128.1 48.0 %collective-permute-start = (bf16[512,512]{1,0:T(8,128)(2,1)}, bf16[512,512]{1,0:T(8,128)(2,1)}, u32[]{:S(2)}, u32[]{:S(2)}) collective-permute-start(bf16[512,512]{1,0:T(8,128)(2,1)} %get-tuple-element.8), channel_id=1, source_target_pairs={{0,8},{4,12},{8,16},{12,20},{16,24},{20,28},{1,9},{5,13},{9,17},{1... | collective-permute-start | bytes 1572872 | tf_op jit(solution)/shard_map/ppermute | solution.py:18
  130.0 46.0 %collective-permute-start.1 = (bf16[512,512]{1,0:T(8,128)(2,1)}, bf16[512,512]{1,0:T(8,128)(2,1)}, u32[]{:S(2)}, u32[]{:S(2)}) collective-permute-start(bf16[512,512]{1,0:T(8,128)(2,1)} %get-tuple-element.8), channel_id=1, source_target_pairs={{0,4},{4,8},{8,12},{12,16},{16,20},{20,24},{24,28},{1,5},{5,9},{9,... | collective-permute-start | bytes 1572872 | tf_op jit(solution)/shard_map/ppermute | solution.py:18
  152.4 10.6 %copy-start.1 = (bf16[1536,4,128]{2,1,0:T(4,128)(2,1)S(1)}, bf16[1536,4,128]{2,1,0:T(4,128)(2,1)}, u32[]{:S(2)}) copy-start(bf16[1536,4,128]{2,1,0:T(4,128)(2,1)} %reshape.78) | copy-start | bytes 4718596
  163.0 13.1 %copy-start.3 = (bf16[512,512]{1,0:T(8,128)(2,1)S(1)}, bf16[512,512]{1,0:T(8,128)(2,1)}, u32[]{:S(2)}) copy-start(bf16[512,512]{1,0:T(8,128)(2,1)} %get-tuple-element.8) | copy-start | bytes 1572868
  194.5 1.2 copy-start

commit v2 on v1

--- a/solution.py
+++ b/solution.py
@@ -107,6 +107,8 @@
 
 MESH = pl.DeviceIdType.MESH
 MIB = 1 << 20
+SENDS = 14
+LOG2_E = 1.4426950408889634
 
 
 class Place:
@@ -120,7 +122,10 @@
         self.to_c = {"seq": self.y, "row": self.x * 2 + 1 - self.c, "col": self.z}
         self.up = {"seq": self.y, "row": row, "col": self.z + 1}
         self.down = {"seq": self.y, "row": row, "col": self.z - 1}
+        self.to_d = {"seq": 1 - self.y, "row": (1 - self.x) * 2 + self.c, "col": self.z}
         self.chip = self.y * 2 + self.x
+        after = (self.chip + 1) % 4
+        self.after = {"seq": after // 2, "row": (after % 2) * 2 + self.c, "col": self.z}
         self.chip_x = self.y * 2 + 1 - self.x
         self.chip_y = (1 - self.y) * 2 + self.x
         self.chip_d = (1 - self.y) * 2 + 1 - self.x
@@ -128,7 +133,7 @@
 
 def barrier(at):
     sem = pltpu.get_barrier_semaphore()
-    for device in (at.to_x, at.to_y, at.to_c):
+    for device in (at.to_x, at.to_y, at.to_c, at.to_d):
         pl.semaphore_signal(sem, inc=1, device_id=device, device_id_type=MESH)
 
     @pl.when(at.z < 3)
@@ -139,62 +144,62 @@
     def _():
         pl.semaphore_signal(sem, inc=1, device_id=at.down, device_id_type=MESH)
 
-    peers = 3 + (at.z < 3).astype(jnp.int32) + (at.z > 0).astype(jnp.int32)
+    peers = 4 + (at.z < 3).astype(jnp.int32) + (at.z > 0).astype(jnp.int32)
     pl.semaphore_wait(sem, peers)
 
 
 class Line:
-    def __init__(self, at, buf, send, recv):
-        self.at, self.buf, self.send, self.recv = at, buf, send, recv
-        self.half = buf.shape[1] // 2
-
-    def copy(self, block, half, way):
-        part = self.buf.at[block, pl.ds(half * self.half, self.half)]
+    def __init__(self, at, part, send, recv):
+        self.at, self.part, self.send, self.recv = at, part, send, recv
+
+    def copy(self, block, part, way):
+        piece = self.part(block, part)
         return pltpu.make_async_remote_copy(
-            src_ref=part, dst_ref=part,
-            send_sem=self.send.at[way, block, half], recv_sem=self.recv.at[block, half],
+            src_ref=piece, dst_ref=piece,
+            send_sem=self.send.at[way, block, part], recv_sem=self.recv.at[block, part],
             device_id=self.at.up if way == 0 else self.at.down, device_id_type=MESH)
 
-    def start(self, half):
+    def start(self, part):
         at = self.at
 
         @pl.when(at.z < 3)
         def _():
-            self.copy(at.z, half, 0).start()
+            self.copy(at.z, part, 0).start()
 
         @pl.when(at.z > 0)
         def _():
-            self.copy(at.z, half, 1).start()
-
-    def step(self, s, half):
+            self.copy(at.z, part, 1).start()
+
+    def step(self, s, part):
         at = self.at
 
         @pl.when(at.z - s >= 0)
         def _():
-            self.copy(at.z - s, half, 0).wait_recv()
+            self.copy(at.z - s, part, 0).wait_recv()
 
             @pl.when(at.z < 3)
             def _():
-                self.copy(at.z - s, half, 0).start()
+                self.copy(at.z - s, part, 0).start()
 
         @pl.when(at.z + s <= 3)
         def _():
-            self.copy(at.z + s, half, 1).wait_recv()
+            self.copy(at.z + s, part, 1).wait_recv()
 
             @pl.when(at.z > 0)
             def _():
-                self.copy(at.z + s, half, 1).start()
-
-    def finish(self, half):
+                self.copy(at.z + s, part, 1).start()
+
+    def finish(self, parts):
         at = self.at
         for s in range(4):
-            @pl.when((at.z - s >= 0) & (at.z < 3))
-            def _():
-                self.copy(at.z - s, half, 0).wait_send()
-
-            @pl.when((at.z + s <= 3) & (at.z > 0))
-            def _():
-                self.copy(at.z + s, half, 1).wait_send()
+            for part in range(parts):
+                @pl.when((at.z - s >= 0) & (at.z < 3))
+                def _():
+                    self.copy(at.z - s, part, 0).wait_send()
+
+                @pl.when((at.z + s <= 3) & (at.z > 0))
+                def _():
+                    self.copy(at.z + s, part, 1).wait_send()
 
 
 class Plane:
@@ -262,33 +267,126 @@
             one.wait_send()
 
 
-SENDS = 14
-
-
-def multiply(chunk, x_all, w_all, total):
+class Halo:
+    def __init__(self, at, kv, rows, sems):
+        self.at, self.kv, self.rows, self.sems = at, kv, rows, sems
+
+    def piece(self, block, h):
+        cols = pl.ds(pl.multiple_of(h * 256, 256), 256)
+        return self.kv.at[pl.ds(block * self.rows, self.rows), cols]
+
+    def on(self, h):
+        return pltpu.make_async_remote_copy(
+            src_ref=self.piece(2, h), dst_ref=self.piece(0, h),
+            send_sem=self.sems.at[0, h], recv_sem=self.sems.at[1, h],
+            device_id=self.at.after, device_id_type=MESH)
+
+    def across(self, block, h):
+        return pltpu.make_async_remote_copy(
+            src_ref=self.piece(block, h), dst_ref=self.piece(1, h),
+            send_sem=self.sems.at[2, h], recv_sem=self.sems.at[3, h],
+            device_id=self.at.to_c, device_id_type=MESH)
+
+    def start(self, h):
+        @pl.when(self.at.chip < 3)
+        def _():
+            self.on(h).start()
+
+        @pl.when(self.at.c == 0)
+        def _():
+            self.across(2, h).start()
+
+    def need(self, h):
+        at = self.at
+
+        @pl.when(at.chip > 0)
+        def _():
+            self.on(h).wait_recv()
+
+            @pl.when(at.c == 1)
+            def _():
+                self.across(0, h).start()
+
+        @pl.when((at.chip > 0) | (at.c == 1))
+        def _():
+            self.across(0, h).wait_recv()
+
+    def finish(self, h):
+        at = self.at
+
+        @pl.when(at.chip < 3)
+        def _():
+            self.on(h).wait_send()
+
+        @pl.when((at.chip > 0) | (at.c == 0))
+        def _():
+            self.across(0, h).wait_send()
+
+
+def multiply(chunk, x_all, w_all, total, low, high):
     depth = x_all.shape[2]
-    width = total.shape[1]
     rows = pl.ds(pl.multiple_of(chunk * depth, 32), depth)
-    tiles = width // 256
+    tiles = (high - low) // 256
 
     @pl.loop(0, tiles)
     def _(tile):
-        cols = pl.ds(pl.multiple_of(tile * 256, 256), 256)
+        cols = pl.ds(pl.multiple_of(low + tile * 256, 256), 256)
         total[:, cols] += jnp.dot(
             x_all[chunk], w_all[rows, cols], preferred_element_type=jnp.float32)
 
-    if width % 256:
-        rest = pl.ds(tiles * 256, width % 256)
+    if (high - low) % 256:
+        rest = pl.ds(low + tiles * 256, (high - low) % 256)
         total[:, rest] += jnp.dot(
             x_all[chunk], w_all[rows, rest], preferred_element_type=jnp.float32)
 
 
-def gather_multiply(at, line, plane, total):
-    late = lambda j: (j == at.chip_d) | (j - at.z == 3) | (at.z - j == 3)
+def kernel(x, wq, wk, wv, wo, gains, cosine, sine, out,
+           x_all, w_all, total, o_all, mixed, kv, q,
+           zs, zr, ps, pr, ms, mr, os, orr, hs, local):
+    at = Place()
+    rows = x.shape[0]
+    nq, nk = wq.shape[1], wk.shape[1]
+    features = wo.shape[1]
+    heads = nk // 128
+    shard, shard_o = w_all.shape[0] // 8, o_all.shape[0] // 8
+    device = at.chip * 2 + at.c
+    mine = pl.ds(pl.multiple_of(device * shard, 16), shard)
+    mine_o = pl.ds(pl.multiple_of(device * shard_o, 16), shard_o)
+    loads = [
+        pltpu.make_async_copy(x, x_all.at[at.z], local.at[0]),
+        pltpu.make_async_copy(wq, w_all.at[mine, pl.ds(0, nq)], local.at[1]),
+        pltpu.make_async_copy(wk, w_all.at[mine, pl.ds(nq, nk)], local.at[2]),
+        pltpu.make_async_copy(wv, w_all.at[mine, pl.ds(nq + nk, nk)], local.at[3]),
+    ]
+    load_o = pltpu.make_async_copy(wo, o_all.at[mine_o], local.at[4])
+    for load in loads:
+        load.start()
+    barrier(at)
+    for load in loads:
+        load.wait()
+    load_o.start()
+    half = rows // 2
+    line = Line(at, lambda b, p: x_all.at[b, pl.ds(p * half, half)], zs, zr)
+    line_m = Line(at, lambda b, p: mixed.at[b, :, pl.ds(p * 256, 256)], ms, mr)
+    plane, plane_o = Plane(at, w_all, ps, pr), Plane(at, o_all, os, orr)
+    halo = Halo(at, kv, rows, hs)
+
+    def late(j):
+        return (j == at.chip_d) | (j - at.z == 3) | (at.z - j == 3)
+
     line.start(0)
     plane.start()
     line.start(1)
     total[...] = jnp.zeros_like(total)
+
+    @pl.when(at.chip == 0)
+    def _():
+        kv[pl.ds(0, rows), :] = jnp.zeros((rows, 2 * nk), jnp.bfloat16)
+
+        @pl.when(at.c == 0)
+        def _():
+            kv[pl.ds(rows, rows), :] = jnp.zeros((rows, 2 * nk), jnp.bfloat16)
+
     line.step(1, 0)
     plane.first()
     line.step(1, 1)
@@ -300,44 +398,18 @@
     def _(j):
         @pl.when(jnp.logical_not(late(j)))
         def _():
-            multiply(j, line.buf, plane.buf, total)
+            multiply(j, x_all, w_all, total, 0, nq + 2 * nk)
 
     line.step(3, 0)
     line.step(3, 1)
     plane.third()
 
-    @pl.loop(0, 4)
-    def _(j):
-        @pl.when(late(j))
-        def _():
-            multiply(j, line.buf, plane.buf, total)
-
-
-def finish(line, plane):
-    line.finish(0)
-    line.finish(1)
-    plane.finish()
-
-
-def project_kernel(x, wq, wk, wv, gains, cosine, sine, q, k, v,
-                   x_all, w_all, total, zs, zr, ps, pr, local):
-    at = Place()
-    shard = w_all.shape[0] // 8
-    nq, nk = wq.shape[1], wk.shape[1]
-    mine = pl.ds(pl.multiple_of((at.chip * 2 + at.c) * shard, 16), shard)
-    loads = [
-        pltpu.make_async_copy(x, x_all.at[at.z], local.at[0]),
-        pltpu.make_async_copy(wq, w_all.at[mine, pl.ds(0, nq)], local.at[1]),
-        pltpu.make_async_copy(wk, w_all.at[mine, pl.ds(nq, nk)], local.at[2]),
-        pltpu.make_async_copy(wv, w_all.at[mine, pl.ds(nq + nk, nk)], local.at[3]),
-    ]
-    for load in loads:
-        load.start()
-    barrier(at)
-    for load in loads:
-        load.wait()
-    line, plane = Line(at, x_all, zs, zr), Plane(at, w_all, ps, pr)
-    gather_multiply(at, line, plane, total)
+    def late_columns(low, high):
+        @pl.loop(0, 4)
+        def _(j):
+            @pl.when(late(j))
+            def _():
+                multiply(j, x_all, w_all, total, low, high)
 
     def head(col, gain):
         block = total[:, pl.ds(pl.multiple_of(col, 128), 128)]
@@ -346,52 +418,94 @@
         turned = normed * cosine[...] + pltpu.roll(normed, 64, 1) * sine[...]
         return turned.astype(jnp.bfloat16)
 
+    late_columns(nq, nq + 2 * nk)
+    own = pl.ds(2 * rows, rows)
+
+    @pl.loop(0, heads)
+    def _(h):
+        kv[own, pl.ds(pl.multiple_of(h * 256, 256), 128)] = head(nq + h * 128, gains[1:2, :])
+        values = total[:, pl.ds(pl.multiple_of(nq + nk + h * 128, 128), 128)]
+        kv[own, pl.ds(pl.multiple_of(h * 256 + 128, 128), 128)] = values.astype(jnp.bfloat16)
+        halo.start(h)
+
+    late_columns(0, nq)
+
     @pl.loop(0, nq // 128)
     def _(h):
         q[:, pl.ds(pl.multiple_of(h * 128, 128), 128)] = head(h * 128, gains[0:1, :])
 
-    @pl.loop(0, nk // 128)
-    def _(h):
-        k[:, pl.ds(pl.multiple_of(h * 128, 128), 128)] = head(nq + h * 128, gains[1:2, :])
-
-    v[...] = total[:, nq + nk:].astype(jnp.bfloat16)
-    finish(line, plane)
-
-
-def output_kernel(x, w, out, x_all, w_all, total, zs, zr, ps, pr, local):
-    at = Place()
-    shard = w_all.shape[0] // 8
-    mine = pl.ds(pl.multiple_of((at.chip * 2 + at.c) * shard, 16), shard)
-    loads = [
-        pltpu.make_async_copy(x, x_all.at[at.z], local.at[0]),
-        pltpu.make_async_copy(w, w_all.at[mine], local.at[1]),
-    ]
-    for load in loads:
-        load.start()
-    barrier(at)
-    for load in loads:
-        load.wait()
-    line, plane = Line(at, x_all, zs, zr), Plane(at, w_all, ps, pr)
-    gather_multiply(at, line, plane, total)
-    out[...] = total[...].astype(jnp.bfloat16)
-    finish(line, plane)
-
-
-def gather_scratch(rows, depth, width):
-    return [
-        pltpu.VMEM((4, rows, depth), jnp.bfloat16),
-        pltpu.VMEM((4 * depth, width), jnp.bfloat16),
-        pltpu.VMEM((rows, width), jnp.float32),
-        pltpu.SemaphoreType.DMA((2, 4, 2)),
-        pltpu.SemaphoreType.DMA((4, 2)),
-        pltpu.SemaphoreType.DMA((SENDS,)),
-        pltpu.SemaphoreType.DMA((8, 2)),
-        pltpu.SemaphoreType.DMA((4,)),
-    ]
-
-
-HBM = pl.BlockSpec(memory_space=pl.ANY)
-LOCAL = pl.BlockSpec(memory_space=pltpu.VMEM)
+    span = half + 2 * rows
+    for tile in range(2):
+        query = lax.broadcasted_iota(jnp.int32, (half, span), 0)
+        key = lax.broadcasted_iota(jnp.int32, (half, span), 1)
+        low = 2 * rows - device * rows - tile * half
+        valid = (key > query) & (key <= query + WINDOW_KEYS) & (key >= low)
+        total[pl.ds(tile * half, half), 0:span] = jnp.where(valid, 0.0, -1e30)
+
+    def attend_head(h):
+        @pl.loop(0, 2)
+        def _(tile):
+            first = pl.multiple_of(tile * half, half)
+            keys = kv[pl.ds(first, span), h * 256:h * 256 + 128]
+            values = kv[pl.ds(first, span), h * 256 + 128:h * 256 + 256]
+            for g in range(2):
+                cols = slice((2 * h + g) * 128, (2 * h + g + 1) * 128)
+                scores = lax.dot_general(
+                    q[pl.ds(first, half), cols], keys, (((1,), (1,)), ((), ())),
+                    preferred_element_type=jnp.float32)
+                scores = scores + total[pl.ds(first, half), 0:span]
+                top = jnp.max(scores, axis=-1, keepdims=True)
+                weights = jnp.exp2((scores - top) * (query_scale * LOG2_E))
+                inverse = 1.0 / jnp.sum(weights, axis=-1, keepdims=True)
+                weights = (weights * inverse).astype(jnp.bfloat16)
+                mixed[at.z, pl.ds(first, half), cols] = jnp.dot(
+                    weights, values, preferred_element_type=jnp.float32).astype(jnp.bfloat16)
+
+    for h in range(heads):
+        halo.need(h)
+        if h == heads - 1:
+            load_o.wait()
+            plane_o.start()
+        attend_head(h)
+        line_m.start(h)
+        if h > 0:
+            line_m.step(1, h - 1)
+
+    total[:, 0:features] = jnp.zeros((rows, features), jnp.float32)
+    line_m.step(1, heads - 1)
+    line_m.step(2, 0)
+    plane_o.first()
+    line_m.step(2, 1)
+    line_m.step(2, 2)
+    plane_o.second()
+    line_m.step(2, 3)
+    plane_o.third()
+
+    def near(j):
+        return (j - at.z < 3) & (at.z - j < 3)
+
+    @pl.loop(0, 4)
+    def _(j):
+        @pl.when(near(j))
+        def _():
+            multiply(j, mixed, o_all, total, 0, features)
+
+    for part in range(heads):
+        line_m.step(3, part)
+
+    @pl.loop(0, 4)
+    def _(j):
+        @pl.when(jnp.logical_not(near(j)))
+        def _():
+            multiply(j, mixed, o_all, total, 0, features)
+
+    out[...] = total[:, 0:features].astype(jnp.bfloat16)
+    line.finish(2)
+    line_m.finish(heads)
+    plane.finish()
+    plane_o.finish()
+    for h in range(heads):
+        halo.finish(h)
 
 
 def angles_of(positions):
@@ -404,39 +518,33 @@
 def fused(tokens, w_query, key_weight, value_weight, w_output, query_gain, key_gain):
     rows, depth = tokens.shape
     nq, nk = w_query.shape[1], key_weight.shape[1]
+    features = w_output.shape[1]
     base = lax.axis_index(("seq", "row")) * rows
-    positions = base + jnp.arange(rows, dtype=jnp.int32)
-    cosine, sine = angles_of(positions)
+    cosine, sine = angles_of(base + jnp.arange(rows, dtype=jnp.int32))
     gains = jnp.stack([query_gain, key_gain])
-    bf16 = jnp.bfloat16
-    queries, key_flat, value_flat = pl.pallas_call(
-        project_kernel,
-        out_shape=[jax.ShapeDtypeStruct((rows, n), bf16) for n in (nq, nk, nk)],
-        in_specs=[HBM] * 4 + [LOCAL] * 3,
-        out_specs=[LOCAL] * 3,
-        scratch_shapes=gather_scratch(rows, depth, nq + 2 * nk),
+    hbm = pl.BlockSpec(memory_space=pl.ANY)
+    vmem = pl.BlockSpec(memory_space=pltpu.VMEM)
+    bf16, dma = jnp.bfloat16, pltpu.SemaphoreType.DMA
+    return pl.pallas_call(
+        kernel,
+        out_shape=jax.ShapeDtypeStruct((rows, features), bf16),
+        in_specs=[hbm] * 5 + [vmem] * 3,
+        out_specs=vmem,
+        scratch_shapes=[
+            pltpu.VMEM((4, rows, depth), bf16),
+            pltpu.VMEM((4 * depth, nq + 2 * nk), bf16),
+            pltpu.VMEM((rows, nq + 2 * nk), jnp.float32),
+            pltpu.VMEM((4 * nq, features), bf16),
+            pltpu.VMEM((4, rows, nq), bf16),
+            pltpu.VMEM((3 * rows, 2 * nk), bf16),
+            pltpu.VMEM((rows, nq), bf16),
+            dma((2, 4, 2)), dma((4, 2)), dma((SENDS,)), dma((8, 2)),
+            dma((2, 4, 4)), dma((4, 4)), dma((SENDS,)), dma((8, 2)),
+            dma((4, 4)), dma((5,)),
+        ],
         compiler_params=pltpu.CompilerParams(
-            collective_id=0, has_side_effects=True, vmem_limit_bytes=56 * MIB),
-    )(tokens, w_query, key_weight, value_weight, gains, cosine, sine)
-    kv_heads = nk // HEAD_SIZE
-    one = shifted((key_flat, value_flat), ("seq", "row"), 1)
-    two = shifted((key_flat, value_flat), ("seq", "row"), 2)
-    key_rows = jnp.concatenate([two[0], one[0], key_flat], 0)
-    value_rows = jnp.concatenate([two[1], one[1], value_flat], 0)
-    kpos = base - 2 * rows + jnp.arange(3 * rows, dtype=jnp.int32)
-    mixed = attend(
-        queries.reshape(rows, nq // HEAD_SIZE, HEAD_SIZE),
-        key_rows.reshape(3 * rows, kv_heads, HEAD_SIZE),
-        value_rows.reshape(3 * rows, kv_heads, HEAD_SIZE), positions, kpos)
-    return pl.pallas_call(
-        output_kernel,
-        out_shape=jax.ShapeDtypeStruct((rows, w_output.shape[1]), bf16),
-        in_specs=[HBM] * 2,
-        out_specs=LOCAL,
-        scratch_shapes=gather_scratch(rows, nq, w_output.shape[1]),
-        compiler_params=pltpu.CompilerParams(
-            collective_id=1, has_side_effects=True, vmem_limit_bytes=48 * MIB),
-    )(mixed, w_output)
+            collective_id=0, has_side_effects=True, vmem_limit_bytes=62 * MIB),
+    )(tokens, w_query, key_weight, value_weight, w_output, gains, cosine, sine)
 
 
 def solution(mesh):

time: 277 us -> 208 us (0.75)
  the two profiles are of different devices: /device:TPU:5 before, /device:TPU:17 now
where the time goes in v2:
time: 208 us; the launch traced here: 205 us
  Pallas kernels  196 us (94%)
  local copies, waits for them, and re-layouts  5.57 us (3%)
  other arithmetic  3.37 us (2%)
    pallas_call x1, Pallas kernels, fused(): pl.pallas_call(kernel, out_shape=jax.ShapeDtypeStruct((rows, features), b...  196 us

profile of v2, /device:TPU:17, one launch (start us, length us, event | category | flops | bytes accessed | tf_op | source)
XLA Modules:
  0.0 205.2 jit_solution(4546000406546060798)
XLA Ops:
  0.0 0.0 copy-start
  0.0 1.4 pad_maximum_fusion.2.gains
  1.4 1.0 fusion
  2.4 1.0 pad_maximum_fusion
  3.4 0.0 copy-done
  3.4 0.0 copy-start.1
  3.4 1.5 copy.8.x
  4.9 0.0 copy-done.1
  4.9 1.5 copy.9.wo
  6.5 196.3 %shard_map.73 = bf16[512,1344]{1,0:T(8,128)(2,1)} custom-call(bf16[512,1344]{1,0:T(8,128)(2,1)} %copy.8.x, bf16[672,1024]{1,0:T(8,128)(2,1)} %wq.1, bf16[672,512]{1,0:T(8,128)(2,1)} %wk.1, bf16[672,512]{1,0:T(8,128)(2,1)} %wv.1, bf16[512,1344]{1,0:T(8,128)(2,1)} %copy.9.wo, f32[2,128]{1,0:T(2,128)} %pad_maximum_fusion.2.gains, ...), custom_call_target="tpu_custom_call" | custom-call | tf_op jit(solution)/shard_map/pallas_call | solution.py:528
  202.8 2.5 %copy.10 = bf16[512,1344]{0,1:T(8,128)(2,1)} copy(bf16[512,1344]{1,0:T(8,128)(2,1)} %shard_map.73) | data formatting | bytes 2752512 | tf_op jit(solution)/shard_map/pallas_call | solution.py:528
  (2 shorter events, 0.0 us)
Async XLA Ops:
  0.0 3.4 %copy-start = (bf16[512,1344]{0,1:T(8,128)(2,1)S(1)}, bf16[512,1344]{0,1:T(8,128)(2,1)}, u32[]{:S(2)}) copy-start(bf16[512,1344]{0,1:T(8,128)(2,1)} %param.7) | copy-start | bytes 4128772
  3.4 1.5 copy-start.1

commit v3 on v2

--- a/solution.py
+++ b/solution.py
@@ -203,17 +203,14 @@
 
 
 class Plane:
-    def __init__(self, at, buf, send, recv):
-        self.at, self.buf, self.send, self.recv = at, buf, send, recv
-        self.rows = buf.shape[0] // 8
-        self.half = self.rows // 2
+    def __init__(self, at, part, send, recv):
+        self.at, self.part, self.send, self.recv = at, part, send, recv
         self.sent = []
 
     def copy(self, chip, core, half, device, slot):
-        start = pl.multiple_of((chip * 2 + core) * self.rows + half * self.half, 16)
-        part = self.buf.at[pl.ds(start, self.half)]
+        piece = self.part(chip * 2 + core, half)
         return pltpu.make_async_remote_copy(
-            src_ref=part, dst_ref=part,
+            src_ref=piece, dst_ref=piece,
             send_sem=self.send.at[slot], recv_sem=self.recv.at[chip * 2 + core, half],
             device_id=device, device_id_type=MESH)
 
@@ -323,42 +320,24 @@
             self.across(0, h).wait_send()
 
 
-def multiply(chunk, x_all, w_all, total, low, high):
-    depth = x_all.shape[2]
-    rows = pl.ds(pl.multiple_of(chunk * depth, 32), depth)
-    tiles = (high - low) // 256
-
-    @pl.loop(0, tiles)
-    def _(tile):
-        cols = pl.ds(pl.multiple_of(low + tile * 256, 256), 256)
-        total[:, cols] += jnp.dot(
-            x_all[chunk], w_all[rows, cols], preferred_element_type=jnp.float32)
-
-    if (high - low) % 256:
-        rest = pl.ds(low + tiles * 256, (high - low) % 256)
-        total[:, rest] += jnp.dot(
-            x_all[chunk], w_all[rows, rest], preferred_element_type=jnp.float32)
-
-
-def kernel(x, wq, wk, wv, wo, gains, cosine, sine, out,
-           x_all, w_all, total, o_all, mixed, kv, q,
-           zs, zr, ps, pr, ms, mr, os, orr, hs, local):
+def kernel(x, wq, wk, wv, wo, gain_q, gain_k, cosine, sine, out,
+           x_all, w_all, total, turned_x, o_all, mixed, kv, q, total_o,
+           zs, zr, ks, kr, qs, qr, ms, mr, os, orr, hs, local):
     at = Place()
-    rows = x.shape[0]
+    depth, rows = x.shape
     nq, nk = wq.shape[1], wk.shape[1]
-    features = wo.shape[1]
+    features = wo.shape[0]
     heads = nk // 128
-    shard, shard_o = w_all.shape[0] // 8, o_all.shape[0] // 8
+    shard = depth // 2
     device = at.chip * 2 + at.c
     mine = pl.ds(pl.multiple_of(device * shard, 16), shard)
-    mine_o = pl.ds(pl.multiple_of(device * shard_o, 16), shard_o)
     loads = [
         pltpu.make_async_copy(x, x_all.at[at.z], local.at[0]),
         pltpu.make_async_copy(wq, w_all.at[mine, pl.ds(0, nq)], local.at[1]),
         pltpu.make_async_copy(wk, w_all.at[mine, pl.ds(nq, nk)], local.at[2]),
         pltpu.make_async_copy(wv, w_all.at[mine, pl.ds(nq + nk, nk)], local.at[3]),
     ]
-    load_o = pltpu.make_async_copy(wo, o_all.at[mine_o], local.at[4])
+    load_o = pltpu.make_async_copy(wo, o_all.at[device], local.at[4])
     for load in loads:
         load.start()
     barrier(at)
@@ -366,18 +345,48 @@
         load.wait()
     load_o.start()
     half = rows // 2
-    line = Line(at, lambda b, p: x_all.at[b, pl.ds(p * half, half)], zs, zr)
+    wide = features // 2
+
+    def weight_part(low, width):
+        def part(index, h):
+            start = pl.multiple_of(index * shard + h * (shard // 2), 16)
+            return w_all.at[pl.ds(start, shard // 2), pl.ds(low, width)]
+        return part
+
+    line = Line(at, lambda b, p: x_all.at[b, pl.ds(p * shard, shard)], zs, zr)
     line_m = Line(at, lambda b, p: mixed.at[b, :, pl.ds(p * 256, 256)], ms, mr)
-    plane, plane_o = Plane(at, w_all, ps, pr), Plane(at, o_all, os, orr)
+    plane_k = Plane(at, weight_part(nq, 2 * nk), ks, kr)
+    plane_q = Plane(at, weight_part(0, nq), qs, qr)
+    plane_o = Plane(at, lambda i, h: o_all.at[i, pl.ds(h * wide, wide)], os, orr)
     halo = Halo(at, kv, rows, hs)
 
-    def late(j):
-        return (j == at.chip_d) | (j - at.z == 3) | (at.z - j == 3)
+    def far(j):
+        return (j - at.z == 3) | (at.z - j == 3)
+
+    def project(j, p, low, high):
+        turned_x[...] = x_all[j, p * shard:(p + 1) * shard, :].T
+        start = pl.multiple_of((j * 2 + p) * shard, 16)
+
+        @pl.loop(0, (high - low) // 256)
+        def _(tile):
+            cols = pl.ds(pl.multiple_of(low + tile * 256, 256), 256)
+            total[:, cols] += jnp.dot(
+                turned_x[...], w_all[pl.ds(start, shard), cols],
+                preferred_element_type=jnp.float32)
+
+    def project_some(which, parts, low, high):
+        @pl.loop(0, 4)
+        def _(j):
+            @pl.when(which(j))
+            def _():
+                for p in parts:
+                    project(j, p, low, high)
 
     line.start(0)
-    plane.start()
+    plane_k.start()
     line.start(1)
     total[...] = jnp.zeros_like(total)
+    total_o[...] = jnp.zeros_like(total_o)
 
     @pl.when(at.chip == 0)
     def _():
@@ -387,29 +396,18 @@
         def _():
             kv[pl.ds(rows, rows), :] = jnp.zeros((rows, 2 * nk), jnp.bfloat16)
 
+    plane_k.first()
+    plane_q.start()
     line.step(1, 0)
-    plane.first()
+    plane_k.second()
     line.step(1, 1)
     line.step(2, 0)
+    plane_k.third()
     line.step(2, 1)
-    plane.second()
-
-    @pl.loop(0, 4)
-    def _(j):
-        @pl.when(jnp.logical_not(late(j)))
-        def _():
-            multiply(j, x_all, w_all, total, 0, nq + 2 * nk)
-
-    line.step(3, 0)
-    line.step(3, 1)
-    plane.third()
-
-    def late_columns(low, high):
-        @pl.loop(0, 4)
-        def _(j):
-            @pl.when(late(j))
-            def _():
-                multiply(j, x_all, w_all, total, low, high)
+    plane_q.first()
+    project_some(lambda j: jnp.logical_not(far(j)), (0, 1), nq, nq + 2 * nk)
+    plane_q.second()
+    project_some(lambda j: jnp.logical_not(far(j) | (j == at.chip_d)), (0, 1), 0, nq)
 
     def head(col, gain):
         block = total[:, pl.ds(pl.multiple_of(col, 128), 128)]
@@ -418,21 +416,24 @@
         turned = normed * cosine[...] + pltpu.roll(normed, 64, 1) * sine[...]
         return turned.astype(jnp.bfloat16)
 
-    late_columns(nq, nq + 2 * nk)
+    for part in range(2):
+        line.step(3, part)
+        project_some(far, (part,), nq, nq + 2 * nk)
     own = pl.ds(2 * rows, rows)
 
     @pl.loop(0, heads)
     def _(h):
-        kv[own, pl.ds(pl.multiple_of(h * 256, 256), 128)] = head(nq + h * 128, gains[1:2, :])
+        kv[own, pl.ds(pl.multiple_of(h * 256, 256), 128)] = head(nq + h * 128, gain_k[...])
         values = total[:, pl.ds(pl.multiple_of(nq + nk + h * 128, 128), 128)]
         kv[own, pl.ds(pl.multiple_of(h * 256 + 128, 128), 128)] = values.astype(jnp.bfloat16)
         halo.start(h)
 
-    late_columns(0, nq)
+    plane_q.third()
+    project_some(lambda j: far(j) | (j == at.chip_d), (0, 1), 0, nq)
 
     @pl.loop(0, nq // 128)
     def _(h):
-        q[:, pl.ds(pl.multiple_of(h * 128, 128), 128)] = head(h * 128, gains[0:1, :])
+        q[:, pl.ds(pl.multiple_of(h * 128, 128), 128)] = head(h * 128, gain_q[...])
 
     span = half + 2 * rows
     for tile in range(2):
@@ -471,7 +472,14 @@
         if h > 0:
             line_m.step(1, h - 1)
 
-    total[:, 0:features] = jnp.zeros((rows, features), jnp.float32)
+    def output(j, p):
+        @pl.loop(0, 2)
+        def _(tile):
+            some = pl.ds(pl.multiple_of(tile * wide, 32), wide)
+            total_o[some, :] += lax.dot_general(
+                o_all[j * 2 + p, some, :], mixed[j, :, p * (nq // 2):(p + 1) * (nq // 2)],
+                (((1,), (1,)), ((), ())), preferred_element_type=jnp.float32)
+
     line_m.step(1, heads - 1)
     line_m.step(2, 0)
     plane_o.first()
@@ -481,28 +489,28 @@
     line_m.step(2, 3)
     plane_o.third()
 
-    def near(j):
-        return (j - at.z < 3) & (at.z - j < 3)
-
     @pl.loop(0, 4)
     def _(j):
-        @pl.when(near(j))
-        def _():
-            multiply(j, mixed, o_all, total, 0, features)
-
-    for part in range(heads):
-        line_m.step(3, part)
-
-    @pl.loop(0, 4)
-    def _(j):
-        @pl.when(jnp.logical_not(near(j)))
-        def _():
-            multiply(j, mixed, o_all, total, 0, features)
-
-    out[...] = total[:, 0:features].astype(jnp.bfloat16)
+        @pl.when(jnp.logical_not(far(j)))
+        def _():
+            for p in range(2):
+                output(j, p)
+
+    for p in range(2):
+        line_m.step(3, 2 * p)
+        line_m.step(3, 2 * p + 1)
+
+        @pl.loop(0, 4)
+        def _(j):
+            @pl.when(far(j))
+            def _():
+                output(j, p)
+
+    out[...] = total_o[...].astype(jnp.bfloat16)
     line.finish(2)
     line_m.finish(heads)
-    plane.finish()
+    plane_k.finish()
+    plane_q.finish()
     plane_o.finish()
     for h in range(heads):
         halo.finish(h)
@@ -521,30 +529,33 @@
     features = w_output.shape[1]
     base = lax.axis_index(("seq", "row")) * rows
     cosine, sine = angles_of(base + jnp.arange(rows, dtype=jnp.int32))
-    gains = jnp.stack([query_gain, key_gain])
     hbm = pl.BlockSpec(memory_space=pl.ANY)
     vmem = pl.BlockSpec(memory_space=pltpu.VMEM)
     bf16, dma = jnp.bfloat16, pltpu.SemaphoreType.DMA
     return pl.pallas_call(
         kernel,
-        out_shape=jax.ShapeDtypeStruct((rows, features), bf16),
-        in_specs=[hbm] * 5 + [vmem] * 3,
+        out_shape=jax.ShapeDtypeStruct((features, rows), bf16),
+        in_specs=[hbm] * 5 + [vmem] * 4,
         out_specs=vmem,
         scratch_shapes=[
-            pltpu.VMEM((4, rows, depth), bf16),
+            pltpu.VMEM((4, depth, rows), bf16),
             pltpu.VMEM((4 * depth, nq + 2 * nk), bf16),
             pltpu.VMEM((rows, nq + 2 * nk), jnp.float32),
-            pltpu.VMEM((4 * nq, features), bf16),
+            pltpu.VMEM((rows, depth // 2), bf16),
+            pltpu.VMEM((8, features, nq // 2), bf16),
             pltpu.VMEM((4, rows, nq), bf16),
             pltpu.VMEM((3 * rows, 2 * nk), bf16),
             pltpu.VMEM((rows, nq), bf16),
-            dma((2, 4, 2)), dma((4, 2)), dma((SENDS,)), dma((8, 2)),
+            pltpu.VMEM((features, rows), jnp.float32),
+            dma((2, 4, 2)), dma((4, 2)),
+            dma((SENDS,)), dma((8, 2)), dma((SENDS,)), dma((8, 2)),
             dma((2, 4, 4)), dma((4, 4)), dma((SENDS,)), dma((8, 2)),
             dma((4, 4)), dma((5,)),
         ],
         compiler_params=pltpu.CompilerParams(
             collective_id=0, has_side_effects=True, vmem_limit_bytes=62 * MIB),
-    )(tokens, w_query, key_weight, value_weight, w_output, gains, cosine, sine)
+    )(tokens.T, w_query, key_weight, value_weight, w_output.T,
+      query_gain.reshape(1, HEAD_SIZE), key_gain.reshape(1, HEAD_SIZE), cosine, sine).T
 
 
 def solution(mesh):

time: 208 us -> 191 us (0.918); the launches traced: 205 us -> 191 us
  Pallas kernels: 196 us -> 186 us
  local copies, waits for them, and re-layouts: 5.57 us -> 2.51 us
    pallas_call x1, Pallas kernels: 196 us -> 186 us  [fused(): pl.pallas_call(kernel, out_shape=jax.ShapeDtypeStruct((features, rows), b...]
    pallas_call x1 -> x0, local copies, waits for them, and re-layouts: 2.49 us -> none  [fused(): pl.pallas_call(kernel, out_shape=jax.ShapeDtypeStruct((rows, features), b...]
where the time goes in v3:
time: 191 us
  Pallas kernels  186 us (97%)
  local copies, waits for them, and re-layouts  2.51 us (1%)
  other arithmetic  2 us (1%)
    pallas_call x1, Pallas kernels, fused(): pl.pallas_call(kernel, out_shape=jax.ShapeDtypeStruct((features, rows), b...  186 us

profile of v3, /device:TPU:17, one launch (start us, length us, event | category | flops | bytes accessed | tf_op | source)
XLA Modules:
  0.0 190.8 jit_solution(10085096619261388050)
XLA Ops:
  0.0 1.0 fusion
  1.0 1.0 pad_maximum_fusion
  2.0 186.3 %shard_map.73 = bf16[1344,512]{1,0:T(8,128)(2,1)} custom-call(bf16[1344,512]{1,0:T(8,128)(2,1)} %bitcast.6, bf16[672,1024]{1,0:T(8,128)(2,1)} %wq.1, bf16[672,512]{1,0:T(8,128)(2,1)} %wk.1, bf16[672,512]{1,0:T(8,128)(2,1)} %wv.1, bf16[1344,512]{1,0:T(8,128)(2,1)} %bitcast.7, f32[1,128]{1,0:T(1,128)} %bitcast.8, f32[1,128]{1,0:T(1,128)} %bitcast.9, ...), custom_call_target="tpu_custom_call" | custom-call | tf_op jit(solution)/shard_map/pallas_call | solution.py:535
  188.3 2.5 %copy.9 = bf16[512,1344]{0,1:T(8,128)(2,1)} copy(bf16[512,1344]{0,1:T(8,128)(2,1)} %bitcast.5) | data formatting | bytes 2752512
  (2 shorter events, 0.0 us)

commit v4 on v3

--- a/solution.py
+++ b/solution.py
@@ -321,7 +321,7 @@
 
 
 def kernel(x, wq, wk, wv, wo, gain_q, gain_k, cosine, sine, out,
-           x_all, w_all, total, turned_x, o_all, mixed, kv, q, total_o,
+           x_all, w_all, total, turned_x, o_all, mixed, kv, q, total_o, mask,
            zs, zr, ks, kr, qs, qr, ms, mr, os, orr, hs, local):
     at = Place()
     depth, rows = x.shape
@@ -401,6 +401,15 @@
     line.step(1, 0)
     plane_k.second()
     line.step(1, 1)
+
+    span = half + 2 * rows
+    for tile in range(2):
+        query = lax.broadcasted_iota(jnp.int32, (half, span), 0)
+        key = lax.broadcasted_iota(jnp.int32, (half, span), 1)
+        low = 2 * rows - device * rows - tile * half
+        valid = (key > query) & (key <= query + WINDOW_KEYS) & (key >= low)
+        mask[tile] = jnp.where(valid, 0.0, -1e30)
+
     line.step(2, 0)
     plane_k.third()
     line.step(2, 1)
@@ -430,18 +439,6 @@
 
     plane_q.third()
     project_some(lambda j: far(j) | (j == at.chip_d), (0, 1), 0, nq)
-
-    @pl.loop(0, nq // 128)
-    def _(h):
-        q[:, pl.ds(pl.multiple_of(h * 128, 128), 128)] = head(h * 128, gain_q[...])
-
-    span = half + 2 * rows
-    for tile in range(2):
-        query = lax.broadcasted_iota(jnp.int32, (half, span), 0)
-        key = lax.broadcasted_iota(jnp.int32, (half, span), 1)
-        low = 2 * rows - device * rows - tile * half
-        valid = (key > query) & (key <= query + WINDOW_KEYS) & (key >= low)
-        total[pl.ds(tile * half, half), 0:span] = jnp.where(valid, 0.0, -1e30)
 
     def attend_head(h):
         @pl.loop(0, 2)
@@ -454,7 +451,7 @@
                 scores = lax.dot_general(
                     q[pl.ds(first, half), cols], keys, (((1,), (1,)), ((), ())),
                     preferred_element_type=jnp.float32)
-                scores = scores + total[pl.ds(first, half), 0:span]
+                scores = scores + mask[tile]
                 top = jnp.max(scores, axis=-1, keepdims=True)
                 weights = jnp.exp2((scores - top) * (query_scale * LOG2_E))
                 inverse = 1.0 / jnp.sum(weights, axis=-1, keepdims=True)
@@ -463,6 +460,8 @@
                     weights, values, preferred_element_type=jnp.float32).astype(jnp.bfloat16)
 
     for h in range(heads):
+        for g in (2 * h, 2 * h + 1):
+            q[:, g * 128:(g + 1) * 128] = head(g * 128, gain_q[...])
         halo.need(h)
         if h == heads - 1:
             load_o.wait()
@@ -547,6 +546,7 @@
             pltpu.VMEM((3 * rows, 2 * nk), bf16),
             pltpu.VMEM((rows, nq), bf16),
             pltpu.VMEM((features, rows), jnp.float32),
+            pltpu.VMEM((2, rows // 2, rows // 2 + WINDOW_KEYS), jnp.float32),
             dma((2, 4, 2)), dma((4, 2)),
             dma((SENDS,)), dma((8, 2)), dma((SENDS,)), dma((8, 2)),
             dma((2, 4, 4)), dma((4, 4)), dma((SENDS,)), dma((8, 2)),

time: 191 us -> 190 us (level)
  no operation moved by 1% of the time
where the time goes in v4:
time: 190 us
  Pallas kernels  185 us (97%)
  local copies, waits for them, and re-layouts  2.51 us (1%)
  other arithmetic  2 us (1%)
    pallas_call x1, Pallas kernels, fused(): pl.pallas_call(kernel, out_shape=jax.ShapeDtypeStruct((features, rows), b...  185 us

profile of v4, /device:TPU:17, one launch (start us, length us, event | category | flops | bytes accessed | tf_op | source)
XLA Modules:
  0.0 189.8 jit_solution(10856361224885623708)
XLA Ops:
  0.0 1.0 fusion
  1.0 1.0 pad_maximum_fusion
  2.0 185.3 %shard_map.73 = bf16[1344,512]{1,0:T(8,128)(2,1)} custom-call(bf16[1344,512]{1,0:T(8,128)(2,1)} %bitcast.6, bf16[672,1024]{1,0:T(8,128)(2,1)} %wq.1, bf16[672,512]{1,0:T(8,128)(2,1)} %wk.1, bf16[672,512]{1,0:T(8,128)(2,1)} %wv.1, bf16[1344,512]{1,0:T(8,128)(2,1)} %bitcast.7, f32[1,128]{1,0:T(1,128)} %bitcast.8, f32[1,128]{1,0:T(1,128)} %bitcast.9, ...), custom_call_target="tpu_custom_call" | custom-call | tf_op jit(solution)/shard_map/pallas_call | solution.py:534
  187.3 2.5 %copy.9 = bf16[512,1344]{0,1:T(8,128)(2,1)} copy(bf16[512,1344]{0,1:T(8,128)(2,1)} %bitcast.5) | data formatting | bytes 2752512
  (2 shorter events, 0.0 us)
